TPU v7x, 32 devices: a whole 2x2x4 slice. The times are simulated.
32 devices in a mesh: dp: 4 (over x, core), expert: 8 (over z, y).
Axes of the slice: x: 2, y: 2, z: 4, core: 2. Of those that a mesh axis runs over, the one named last changes fastest.
Arguments:
- tokens: bfloat16 [4096, 1024], P(('dp', 'expert')), may hold values from -6 to 6
- expert_ids: int32 [4096, 1], P(('dp', 'expert')), may hold values from 0 to 7; in each aligned block of 128 rows (0 to 127, 128 to 255, ...) at most 48 rows name the same one
- gate_scale: float32 [4096], P(('dp', 'expert')), may hold values from 0.1 to 1
- w_gate_up: bfloat16 [8, 1024, 768], P('expert'), may hold values from -0.1875 to 0.1875
- w_down: bfloat16 [8, 1024, 384], P('expert'), may hold values from -0.3125 to 0.3125
- out_grad: bfloat16 [4096, 1024], P(('dp', 'expert')), may hold values from -1.5 to 1.5
Outputs:
- mixed: bfloat16 [4096, 1024], P(('dp', 'expert'))
- input_rows: bfloat16 [4096, 1024], P(('dp', 'expert'))
- gate_grad_rows: float32 [4096], P(('dp', 'expert'))
- grad_gate_up: float32 [8, 1024, 768], P('expert', 'dp')
- grad_down: float32 [8, 1024, 384], P('expert', 'dp')
Inputs may be any that keep to these rules, and one draw needn't show every extreme that they name: `expert_ids`: among the rows of one device no expert is named more than 48 times, a bound that some block reaches.
All inputs are finite; a program needn't handle non-finite values.
Results may differ from a plain program's by a relative error of at most 0.017.
Values may be sent and summed in bfloat16 or wider, within the bound.
A program may use at most 64 MiB of HBM per device.

v0:
```python
import jax
import jax.numpy as jnp
from jax import lax
from jax.sharding import PartitionSpec as P

BLOCK = 128


def slot_places(route_ids, experts, capacity):
    onehot = (route_ids[:, None] == jnp.arange(experts, dtype=jnp.int32)[None, :]).astype(jnp.int32)
    before = jnp.cumsum(onehot, axis=0) - onehot
    position = jnp.sum(before * onehot, axis=1)
    slot_index = route_ids * capacity + position
    return (slot_index[None, :] == jnp.arange(experts * capacity, dtype=jnp.int32)[:, None]).astype(
        jnp.bfloat16
    )


def contract_rows(left, right):
    return lax.dot_general(
        left, right, (((0,), (0,)), ((), ())), preferred_element_type=jnp.float32
    )


def contract_last(left, right):
    return lax.dot_general(
        left, right, (((1,), (1,)), ((), ())), preferred_element_type=jnp.float32
    )


def expert_forward(slot_rows, weight_in, weight_out):
    hidden_units = weight_out.shape[1]
    gate_up = jnp.dot(slot_rows, weight_in, preferred_element_type=jnp.float32)
    gate_part = gate_up[:, :hidden_units]
    up_part = gate_up[:, hidden_units:]
    hidden = (gate_part * jax.nn.sigmoid(gate_part) * up_part).astype(jnp.bfloat16)
    result = contract_last(hidden, weight_out).astype(jnp.bfloat16)
    return (gate_part, up_part, hidden, result)


def expert_backward(slot_grads, gate_part, up_part, weight_in, weight_out):
    hidden_grad = jnp.dot(slot_grads, weight_out, preferred_element_type=jnp.float32)
    sig_gate = jax.nn.sigmoid(gate_part)
    gate_grad = hidden_grad * up_part * sig_gate * (1.0 + gate_part * (1.0 - sig_gate))
    up_grad = hidden_grad * gate_part * sig_gate
    both_grads = jnp.concatenate([gate_grad, up_grad], axis=1).astype(jnp.bfloat16)
    input_grad = contract_last(both_grads, weight_in).astype(jnp.bfloat16)
    return (both_grads, input_grad)


def pick_entry(table, wanted):
    entries = table.shape[-1]
    chosen = (jnp.arange(entries, dtype=jnp.int32) == wanted).astype(jnp.int32)
    return jnp.sum(table * chosen, axis=-1)


def run_blocks(block_source, grad_source, live_rows, weight_in, weight_out):
    length, model_width = block_source.shape
    hidden_units = weight_out.shape[1]
    start_buffers = (
        jnp.zeros((length, model_width), jnp.bfloat16),
        jnp.zeros((length, model_width), jnp.bfloat16),
        jnp.zeros((length, 2 * hidden_units), jnp.bfloat16),
        jnp.zeros((length, hidden_units), jnp.bfloat16),
    )

    def one_block(block_index, buffers):
        first_row = block_index * BLOCK
        block_rows = lax.dynamic_slice_in_dim(block_source, first_row, BLOCK, 0)
        block_grads = lax.dynamic_slice_in_dim(grad_source, first_row, BLOCK, 0)
        gate_part, up_part, hidden, result = expert_forward(block_rows, weight_in, weight_out)
        both_grads, input_grad = expert_backward(
            block_grads, gate_part, up_part, weight_in, weight_out
        )
        fresh = (result, input_grad, both_grads, hidden)
        return tuple(
            (
                lax.dynamic_update_slice_in_dim(buffer, update, first_row, 0)
                for buffer, update in zip(buffers, fresh)
            )
        )

    block_count = (live_rows + BLOCK - 1) // BLOCK
    return lax.fori_loop(0, block_count, one_block, start_buffers)


def on_device(tokens, expert_ids, gate_scale, w_gate_up, w_down, out_grad):
    row_count, model_width = tokens.shape
    experts = lax.axis_size("expert")
    capacity = 3 * row_count // experts
    slot_count = experts * capacity
    spare_rows = slot_count // 4
    length = slot_count + spare_rows + BLOCK
    route = expert_ids[:, 0]
    expert_range = jnp.arange(experts, dtype=jnp.int32)
    counts = jnp.sum((route[:, None] == expert_range[None, :]).astype(jnp.int32), axis=0)
    count_table = lax.all_gather(counts[None, :], "expert", axis=0, tiled=True)
    home = lax.axis_index("expert")
    my_counts = pick_entry(count_table, home)
    loads = jnp.sum(count_table, axis=0)
    my_load = pick_entry(loads, home)
    places = slot_places(route, experts, capacity)
    scaled = (gate_scale[:, None] * out_grad.astype(jnp.float32)).astype(jnp.bfloat16)
    send_rows = jnp.dot(places, tokens, preferred_element_type=jnp.float32).astype(jnp.bfloat16)
    send_grads = jnp.dot(places, scaled, preferred_element_type=jnp.float32).astype(jnp.bfloat16)
    slot_rows, slot_grads = (
        lax.all_to_all(send_rows, "expert", split_axis=0, concat_axis=0, tiled=True),
        lax.all_to_all(send_grads, "expert", split_axis=0, concat_axis=0, tiled=True),
    )
    starts = jnp.cumsum(my_counts) - my_counts
    ends = starts + my_counts
    position = jnp.arange(length, dtype=jnp.int32)
    sender = jnp.sum((ends[None, :] <= position[:, None]).astype(jnp.int32), axis=1)
    sender = jnp.minimum(sender, experts - 1)
    live = position < my_load
    source = jnp.where(
        live, sender * capacity + position - pick_entry(starts[None, :], sender[:, None]), 0
    )
    compact_rows = jnp.where(
        live[:, None], jnp.take(slot_rows, source, axis=0), jnp.zeros((), jnp.bfloat16)
    )
    compact_grads = jnp.where(
        live[:, None], jnp.take(slot_grads, source, axis=0), jnp.zeros((), jnp.bfloat16)
    )
    weight_in = w_gate_up[0]
    weight_out = w_down[0]
    buffers = run_blocks(compact_rows, compact_grads, my_load, weight_in, weight_out)
    result_buffer, ingrad_buffer, both_buffer, hidden_buffer = buffers
    term_width = both_buffer.shape[1] + hidden_buffer.shape[1]
    all_blocks = (my_load + BLOCK - 1) // BLOCK
    slot_index = jnp.arange(slot_count, dtype=jnp.int32)
    slot_sender = slot_index // capacity
    slot_rank = slot_index % capacity
    slot_live = slot_rank < pick_entry(my_counts[None, :], slot_sender[:, None])
    slot_source = jnp.where(
        slot_live, pick_entry(starts[None, :], slot_sender[:, None]) + slot_rank, 0
    )
    back_result = jnp.where(
        slot_live[:, None],
        jnp.take(result_buffer, slot_source, axis=0),
        jnp.zeros((), jnp.bfloat16),
    )
    back_ingrad = jnp.where(
        slot_live[:, None],
        jnp.take(ingrad_buffer, slot_source, axis=0),
        jnp.zeros((), jnp.bfloat16),
    )
    got_result, got_ingrad = (
        lax.all_to_all(back_result, "expert", split_axis=0, concat_axis=0, tiled=True),
        lax.all_to_all(back_ingrad, "expert", split_axis=0, concat_axis=0, tiled=True),
    )

    def add_block(block_index, running):
        first_row = block_index * BLOCK
        rows_part = lax.dynamic_slice(compact_rows, (first_row, 0), (BLOCK, model_width))
        grads_part = lax.dynamic_slice(compact_grads, (first_row, 0), (BLOCK, model_width))
        both_part = lax.dynamic_slice_in_dim(both_buffer, first_row, BLOCK, 0)
        hidden_part = lax.dynamic_slice_in_dim(hidden_buffer, first_row, BLOCK, 0)
        return running + jnp.concatenate(
            [contract_rows(rows_part, both_part), contract_rows(grads_part, hidden_part)], axis=1
        )

    summed = lax.psum_scatter(
        lax.fori_loop(
            0, all_blocks, add_block, jnp.zeros((model_width, term_width), jnp.float32)
        ).astype(jnp.bfloat16),
        "dp",
        scatter_dimension=0,
        tiled=True,
    ).astype(jnp.float32)
    pair_width = weight_in.shape[1]
    ffn_rows = contract_rows(places, got_result)
    mixed = (gate_scale[:, None] * ffn_rows).astype(jnp.bfloat16)
    gate_grad_rows = jnp.sum(out_grad.astype(jnp.float32) * ffn_rows, axis=1)
    input_rows = contract_rows(places, got_ingrad).astype(jnp.bfloat16)
    return (
        mixed,
        input_rows,
        gate_grad_rows,
        summed[:, :pair_width][None],
        summed[:, pair_width:][None],
    )


def solution(mesh):
    return jax.shard_map(
        on_device,
        mesh=mesh,
        in_specs=(
            P(("dp", "expert"), None),
            P(("dp", "expert"), None),
            P(("dp", "expert")),
            P("expert", None, None),
            P("expert", None, None),
            P(("dp", "expert"), None),
        ),
        out_specs=(
            P(("dp", "expert"), None),
            P(("dp", "expert"), None),
            P(("dp", "expert")),
            P("expert", "dp", None),
            P("expert", "dp", None),
        ),
        check_vma=False,
    )
```

profile of v0, /device:TPU:0, one launch (start us, length us, event | category | flops | bytes accessed | tf_op | source)
XLA Modules:
  0.0 183.9 jit_solution(4433873864724181451)
XLA Ops:
  9.6 2.3 %convolution_convert_fusion.2 = bf16[384,1024]{1,0:T(8,128)(2,1)} fusion(bf16[128,1024]{1,0:T(8,128)(2,1)} %param.19, f32[128]{0:T(128)} %param.16, s32[128]{0:T(128)S(1)} %multiply_add_fusion), kind=kOutput, calls=%fused_computation.31 | convolution fusion | flops 101498880 | bytes 1049600 | tf_op jit(solution)/shard_map/dot_general | solution.py:105
  11.9 7.3 %all-to-all-start.1 = ((bf16[8,48,1024]{2,1,0:T(8,128)(2,1)}), bf16[8,48,1024]{2,1,0:T(8,128)(2,1)S(1)}, u32[]{:S(2)}, u32[]{:S(2)}) async-start(bf16[8,48,1024]{2,1,0:T(8,128)(2,1)} %bitcast.8), calls=%async_computation.1 | async-start | bytes 1572864 | tf_op jit(solution)/shard_map/all_to_all | solution.py:108
  20.5 18.9 %all-to-all-done.1 = bf16[8,48,1024]{2,1,0:T(8,128)(2,1)S(1)} async-done(((bf16[8,48,1024]{2,1,0:T(8,128)(2,1)}), bf16[8,48,1024]{2,1,0:T(8,128)(2,1)S(1)}, u32[]{:S(2)}, u32[]{:S(2)}) %all-to-all-start.1) | async-done | bytes 786464 | tf_op jit(solution)/shard_map/all_to_all | solution.py:108
  39.4 3.6 %all-to-all-start = ((bf16[8,48,1024]{2,1,0:T(8,128)(2,1)}), bf16[8,48,1024]{2,1,0:T(8,128)(2,1)S(1)}, u32[]{:S(2)}, u32[]{:S(2)}) async-start(bf16[8,48,1024]{2,1,0:T(8,128)(2,1)} %bitcast.4), calls=%async_computation | async-start | bytes 1572864 | tf_op jit(solution)/shard_map/all_to_all | solution.py:107
  44.5 19.0 %all-reduce = s32[64]{0:T(128)S(1)} all-reduce(s32[64]{0:T(128)S(1)} %dynamic-update-slice), channel_id=2, replica_groups=mesh['dp'=4,'expert'=8] {'expert'}, use_global_device_ids=true, to_apply=%add | all-reduce | flops 64 | bytes 512
  66.1 2.9 %gather_fusion.1 = bf16[608,1024]{1,0:T(8,128)(2,1)S(1)} fusion(bf16[384,1024]{1,0:T(8,128)(2,1)S(1)} %bitcast.39, s32[1024]{0:T(1024)S(1)} %pad_clamp_fusion.1), kind=kCustom, calls=%fused_computation.2.clone | custom fusion | bytes 2492800 | tf_op jit(solution)/shard_map/jit(_take)/gather | solution.py:123
  69.0 3.5 %gather_fusion = bf16[608,1024]{1,0:T(8,128)(2,1)} fusion(bf16[384,1024]{1,0:T(8,128)(2,1)S(1)} %bitcast.40, s32[1024]{0:T(1024)S(1)} %pad_clamp_fusion.1), kind=kCustom, calls=%fused_computation.clone | custom fusion | bytes 2492800 | tf_op jit(solution)/shard_map/jit(_take)/gather | solution.py:120
  72.5 3.1 %select_select_fusion = (bf16[608,1024]{1,0:T(8,128)(2,1)}, bf16[608,1024]{1,0:T(8,128)(2,1)}) fusion(bf16[608,1024]{1,0:T(8,128)(2,1)S(1)} %gather_fusion.1, pred[608]{0:T(1024)(128)(4,1)S(1)} %get-tuple-element.151, pred[608]{0:T(1024)(128)(4,1)S(1)} %get-tuple-element.161, bf16[608,1024]{1,0:T(8,128)(2,1)} %gather_fusion), kind=kLoop, calls=%fused_computation.33 | loop fusion | flops 2490368 | bytes 4981952 | tf_op jit(solution)/shard_map/jit(_where)/select_n | solution.py:122
  78.3 5.2 %while.26 = (s32[]{:T(128)}, bf16[608,1024]{1,0:T(8,128)(2,1)}, bf16[608,1024]{1,0:T(8,128)(2,1)S(1)}, bf16[608,768]{1,0:T(8,128)(2,1)}, bf16[608,384]{1,0:T(8,1...) while((s32[]{:T(128)}, bf16[608,1024]{1,0:T(8,128)(2,1)}, ...), condition=%wide.region_11.13_spmd, body=%wide.region_10.12_spmd.sunk | while | flops 605962240 | bytes 11174119 | solution.py:84
  78.3 1.4 fusion.67
  79.8 1.3 multiply_convert_fusion.6
  83.6 2.7 %broadcast_in_dim.101 = f32[1024,1152]{0,1:T(8,128)} broadcast(f32[]{:T(128)} %constant.102.clone.1), dimensions={} | broadcast | bytes 4718596 | tf_op jit(solution)/shard_map/broadcast_in_dim | solution.py:165
  86.3 7.0 %while.27 = (s32[]{:T(128)}, f32[1024,1152]{0,1:T(8,128)}, s32[]{:T(128)}, bf16[608,1024]{1,0:T(8,128)(2,1)}, bf16[608,768]{1,0:T(8,128)(2,1)}, /*index=5*/bf16[...) while((s32[]{:T(128)}, f32[1024,1152]{0,1:T(8,128)}, ...), condition=%wide.region_15.18_spmd, body=%wide.region_14.17_spmd.sunk | while | flops 304349184 | bytes 57444560 | solution.py:164
  86.3 1.5 fusion.75
  87.8 1.6 fusion.76
  89.5 1.7 maximum_add_fusion.2
  91.2 2.1 %copy-done.2 = f32[1024,1152]{0,1:T(8,128)} copy-done((f32[1024,1152]{0,1:T(8,128)}, f32[1024,1152]{0,1:T(8,128)S(1)}, u32[]{:S(2)}) %copy-start.2) | copy-done | bytes 4718616 | tf_op jit(solution)/shard_map/while
  93.3 4.9 %copy.12 = bf16[1024,1152]{1,0:T(8,128)(2,1)} copy(f32[1024,1152]{0,1:T(8,128)} %get-tuple-element.105) | data formatting | bytes 7077888 | tf_op jit(solution)/shard_map/while | solution.py:164
  99.5 2.1 %gather_fusion.2 = bf16[384,1024]{1,0:T(8,128)(2,1)S(1)} fusion(bf16[608,1024]{1,0:T(8,128)(2,1)S(1)} %copy-done.4, s32[1024]{0:T(1024)S(1)} %pad_clamp_fusion), kind=kCustom, calls=%fused_computation.1.clone | custom fusion | bytes 1574400 | tf_op jit(solution)/shard_map/jit(_take)/gather | solution.py:140
  101.6 2.1 %gather_fusion.3 = bf16[384,1024]{1,0:T(8,128)(2,1)S(1)} fusion(bf16[608,1024]{1,0:T(8,128)(2,1)S(1)} %get-tuple-element.102, s32[1024]{0:T(1024)S(1)} %pad_clamp_fusion), kind=kCustom, calls=%fused_computation.3.clone | custom fusion | bytes 1574400 | tf_op jit(solution)/shard_map/jit(_take)/gather | solution.py:145
  104.9 44.0 %all_to_all.48 = bf16[8,48,1024]{2,1,0:T(8,128)(2,1)S(1)} all-to-all(bf16[8,48,1024]{2,1,0:T(8,128)(2,1)S(1)} %bitcast.44), channel_id=1, replica_groups=mesh['dp'=4,'expert'=8] {'expert'}, dimensions={0} | all-to-all | bytes 1572864 | tf_op jit(solution)/shard_map/all_to_all | solution.py:150
  148.9 3.7 %all-to-all-start.2 = ((bf16[8,48,1024]{2,1,0:T(8,128)(2,1)}), bf16[8,48,1024]{2,1,0:T(8,128)(2,1)S(1)}, u32[]{:S(2)}, u32[]{:S(2)}) async-start(bf16[8,48,1024]{2,1,0:T(8,128)(2,1)} %bitcast.10), calls=%async_computation.2 | async-start | bytes 1572864 | tf_op jit(solution)/shard_map/all_to_all | solution.py:149
  153.7 18.8 %all-to-all-done.2 = bf16[8,48,1024]{2,1,0:T(8,128)(2,1)S(1)} async-done(((bf16[8,48,1024]{2,1,0:T(8,128)(2,1)}), bf16[8,48,1024]{2,1,0:T(8,128)(2,1)S(1)}, u32[]{:S(2)}, u32[]{:S(2)}) %all-to-all-start.2) | async-done | bytes 786464 | tf_op jit(solution)/shard_map/all_to_all | solution.py:149
  172.5 1.7 fusion.19
  (63 shorter events, 18.1 us)
Async XLA Ops:
  7.2 12.1 %copy-start = (bf16[128,1024]{1,0:T(8,128)(2,1)S(1)}, bf16[128,1024]{1,0:T(8,128)(2,1)}, u32[]{:S(2)}) copy-start(bf16[128,1024]{1,0:T(8,128)(2,1)} %param.14) | copy-start | bytes 786436
  11.9 27.5 %all-to-all-start.1 = ((bf16[8,48,1024]{2,1,0:T(8,128)(2,1)}), bf16[8,48,1024]{2,1,0:T(8,128)(2,1)S(1)}, u32[]{:S(2)}, u32[]{:S(2)}) async-start(bf16[8,48,1024]{2,1,0:T(8,128)(2,1)} %bitcast.8), calls=%async_computation.1 | async-start | bytes 1572864 | tf_op jit(solution)/shard_map/all_to_all | solution.py:108
  19.2 23.8 %copy-start.11 = (u32[32]{0:T(128)S(1)}, u32[32]{0:T(128)}, u32[]{:S(2)}) copy-start(u32[32]{0:T(128)} %constant.107) | copy-start | bytes 388
  39.4 29.6 %all-to-all-start = ((bf16[8,48,1024]{2,1,0:T(8,128)(2,1)}), bf16[8,48,1024]{2,1,0:T(8,128)(2,1)S(1)}, u32[]{:S(2)}, u32[]{:S(2)}) async-start(bf16[8,48,1024]{2,1,0:T(8,128)(2,1)} %bitcast.4), calls=%async_computation | async-start | bytes 1572864 | tf_op jit(solution)/shard_map/all_to_all | solution.py:107
  43.0 131.2 %reduce-scatter.2.cloned.1.call-start = ((), (), s32[]{:S(2)}) async-start(), calls=%async_computation.5 | async-start | bytes 2949120 | tf_op jit(solution)/shard_map/reduce_scatter | solution.py:163
  63.7 2.4 %copy-start.9 = (s32[8]{0:T(128)}, s32[8]{0:T(128)S(1)}, u32[]{:S(2)}) copy-start(s32[8]{0:T(128)S(1)} %get-tuple-element.106) | copy-start | bytes 100
  76.6 1.8 copy-start.3
  78.3 1.4 copy-start.5
  86.3 3.1 %copy-start.1 = (f32[1024,1152]{0,1:T(8,128)S(1)}, f32[1024,1152]{0,1:T(8,128)}, u32[]{:S(2)}) copy-start(f32[1024,1152]{0,1:T(8,128)} %get-tuple-element.330) | copy-start | bytes 14155780 | tf_op jit(solution)/shard_map/while
  91.2 2.1 %copy-start.2 = (f32[1024,1152]{0,1:T(8,128)}, f32[1024,1152]{0,1:T(8,128)S(1)}, u32[]{:S(2)}) copy-start(f32[1024,1152]{0,1:T(8,128)S(1)} %maximum_add_fusion.2) | copy-start | bytes 14155780 | tf_op jit(solution)/shard_map/while
  98.2 0.7 copy-start.10
  98.2 1.3 copy-start.4
  101.6 2.1 %copy-start.8 = (pred[384]{0:T(512)(128)(4,1)S(1)}, pred[384]{0:T(512)(128)(4,1)}, u32[]{:S(2)}) copy-start(pred[384]{0:T(512)(128)(4,1)} %get-tuple-element.150) | copy-start | bytes 1156
  148.9 23.7 %copy-start.6 = (bf16[128,1024]{1,0:T(8,128)(2,1)S(1)}, bf16[128,1024]{1,0:T(8,128)(2,1)}, u32[]{:S(2)}) copy-start(bf16[128,1024]{1,0:T(8,128)(2,1)} %param.19) | copy-start | bytes 786436
  148.9 23.7 %copy-start.7 = (f32[128]{0:T(128)S(1)}, f32[128]{0:T(128)}, u32[]{:S(2)}) copy-start(f32[128]{0:T(128)} %param.16) | copy-start | bytes 1540
  148.9 23.7 %all-to-all-start.2 = ((bf16[8,48,1024]{2,1,0:T(8,128)(2,1)}), bf16[8,48,1024]{2,1,0:T(8,128)(2,1)S(1)}, u32[]{:S(2)}, u32[]{:S(2)}) async-start(bf16[8,48,1024]{2,1,0:T(8,128)(2,1)} %bitcast.10), calls=%async_computation.2 | async-start | bytes 1572864 | tf_op jit(solution)/shard_map/all_to_all | solution.py:149
Sparse Core Ops, SparseCore 0:
  98.4 52.2 reduce-scatter.1
where the time goes:
time: 185 us; the launch traced here: 184 us
  blocking collectives  63 us (34%)
  waiting for transfers between devices  37.8 us (20%)
  local copies, waits for them, and re-layouts  26.4 us (14%)
  between operations  15.5 us (8%)
  starting transfers between devices  14.7 us (8%)
  matrix products  13.8 us (7%)
  other arithmetic  12.7 us (7%)
    all_to_all x1, blocking collectives, on_device(): lax.all_to_all(back_ingrad, 'expert', split_axis=0, concat_axis=0, tiled=...  44 us
    unnamed x1, blocking collectives  19 us
    all_to_all x1, waiting for transfers between devices, on_device(): lax.all_to_all(send_grads, 'expert', split_axis=0, concat_axis=0, tiled=T...  18.9 us
    all_to_all x1, waiting for transfers between devices, on_device(): lax.all_to_all(back_result, 'expert', split_axis=0, concat_axis=0, tiled=...  18.8 us
    all_to_all x1, starting transfers between devices, on_device(): lax.all_to_all(send_grads, 'expert', split_axis=0, concat_axis=0, tiled=T...  7.31 us
    dot_general x4, matrix products, contract_rows(): lax.dot_general(left, right, (((0,), (0,)), ((), ())), preferred_element_...  5.85 us
    while x1, local copies, waits for them, and re-layouts, on_device(): lax.fori_loop(0, all_blocks, add_block, jnp.zeros((model_width, term_widt...  4.93 us
    all_to_all x1, starting transfers between devices, on_device(): lax.all_to_all(back_result, 'expert', split_axis=0, concat_axis=0, tiled=...  3.74 us
  transfers between devices with their start and end apart: 4, of which 2 were waited for; matrix products, arithmetic and copies ran while one was open for 8% of the time, Pallas kernels for 0%

commit v1 on v0

--- a/solution.py
+++ b/solution.py
@@ -4,6 +4,30 @@
 from jax.sharding import PartitionSpec as P
 
 BLOCK = 128
+
+
+def cut_along(x, dim, peers):
+    lengths = x.shape
+    blocks = x.reshape(*lengths[:dim], peers, lengths[dim] // peers, *lengths[dim + 1 :])
+    return jnp.moveaxis(blocks, dim, 0)
+
+
+def laid_out(blocks, dim):
+    blocks = jnp.moveaxis(blocks, 0, dim)
+    shape = blocks.shape
+    return blocks.reshape(*shape[:dim], shape[dim] * shape[dim + 1], *shape[dim + 2 :])
+
+
+def rotated_exchange(x, axis, split_dim, concat_dim):
+    devices, here = (lax.axis_size(axis), lax.axis_index(axis))
+    parts = cut_along(x, split_dim, devices)
+    out = parts
+    for lap in range(1, devices):
+        target, source = ((here + lap) % devices, (here - lap) % devices)
+        sent = lax.dynamic_index_in_dim(parts, target, 0)
+        other = lax.ppermute(sent, axis, [(i, (i + lap) % devices) for i in range(devices)])
+        out = lax.dynamic_update_slice_in_dim(out, other, source, axis=0)
+    return laid_out(out, concat_dim)
 
 
 def slot_places(route_ids, experts, capacity):
@@ -105,7 +129,7 @@
     send_grads = jnp.dot(places, scaled, preferred_element_type=jnp.float32).astype(jnp.bfloat16)
     slot_rows, slot_grads = (
         lax.all_to_all(send_rows, "expert", split_axis=0, concat_axis=0, tiled=True),
-        lax.all_to_all(send_grads, "expert", split_axis=0, concat_axis=0, tiled=True),
+        rotated_exchange(send_grads, "expert", 0, 0),
     )
     starts = jnp.cumsum(my_counts) - my_counts
     ends = starts + my_counts

time: 185 us -> 187 us (1.011)
  waiting for transfers between devices: 37.8 us -> 29.3 us
  starting transfers between devices: 14.7 us -> 20 us
  blocking collectives: 63 us -> 66.6 us
  local copies, waits for them, and re-layouts: 26.4 us -> 28.4 us
    all_to_all x1 -> x0, waiting for transfers between devices: 18.9 us -> none  [on_device(): lax.all_to_all(send_grads, 'expert', split_axis=0, concat_axis=0, tiled=T...]
    ppermute x0 -> x7, starting transfers between devices: none -> 11.4 us  [rotated_exchange(): lax.ppermute(sent, axis, [(i, (i + lap) % devices) for i in range(devices)])]
    ppermute x0 -> x7, waiting for transfers between devices: none -> 10.4 us  [rotated_exchange(): lax.ppermute(sent, axis, [(i, (i + lap) % devices) for i in range(devices)])]
    all_to_all x1 -> x0, starting transfers between devices: 7.31 us -> none  [on_device(): lax.all_to_all(send_grads, 'expert', split_axis=0, concat_axis=0, tiled=T...]
    all_to_all x1, blocking collectives: 44 us -> 48.2 us  [on_device(): lax.all_to_all(back_ingrad, 'expert', split_axis=0, concat_axis=0, tiled=...]
  transfers between devices with their start and end apart: 4 -> 10, of which waited for: 2 -> 3; matrix products, arithmetic and copies ran while one was open for 8% -> 9% of each run, Pallas kernels for 0% -> 0%
where the time goes in v1:
time: 187 us
  blocking collectives  66.6 us (36%)
  waiting for transfers between devices  29.3 us (16%)
  local copies, waits for them, and re-layouts  28.4 us (15%)
  starting transfers between devices  20 us (11%)
  between operations  16 us (9%)
  other arithmetic  13.5 us (7%)
  matrix products  12.9 us (7%)
    all_to_all x1, blocking collectives, on_device(): lax.all_to_all(back_ingrad, 'expert', split_axis=0, concat_axis=0, tiled=...  48.2 us
    all_to_all x1, waiting for transfers between devices, on_device(): lax.all_to_all(back_result, 'expert', split_axis=0, concat_axis=0, tiled=...  18.9 us
    unnamed x1, blocking collectives  18.3 us
    ppermute x7, starting transfers between devices, rotated_exchange(): lax.ppermute(sent, axis, [(i, (i + lap) % devices) for i in range(devices)])  11.4 us
    ppermute x7, waiting for transfers between devices, rotated_exchange(): lax.ppermute(sent, axis, [(i, (i + lap) % devices) for i in range(devices)])  10.4 us
    dot_general x4, matrix products, contract_rows(): lax.dot_general(left, right, (((0,), (0,)), ((), ())), preferred_element_...  5.87 us
    while x1, local copies, waits for them, and re-layouts, on_device(): lax.fori_loop(0, all_blocks, add_block, jnp.zeros((model_width, term_widt...  4.93 us
    all_to_all x1, starting transfers between devices, on_device(): lax.all_to_all(send_rows, 'expert', split_axis=0, concat_axis=0, tiled=True)  4.88 us
  transfers between devices with their start and end apart: 10, of which 3 were waited for; matrix products, arithmetic and copies ran while one was open for 9% of the time, Pallas kernels for 0%

profile of v1, /device:TPU:0, one launch (start us, length us, event | category | flops | bytes accessed | tf_op | source)
XLA Modules:
  0.0 186.6 jit_solution(15124972877308181577)
XLA Ops:
  11.1 3.0 %collective-permute-start = (bf16[1,48,1024]{2,1,0:T(8,128)(2,1)S(1)}, bf16[1,48,1024]{2,1,0:T(8,128)(2,1)S(1)}, u32[]{:S(2)}, u32[]{:S(2)}) collective-permute-start(bf16[1,48,1024]{2,1,0:T(8,128)(2,1)S(1)} %constant_dynamic-slice_fusion.6), channel_id=1, source_target_pairs={{0,1},{1,2},{2,3},{3,4},{4,5},{5,6},{6,7},{7,0},{8,9},{9,10},{10,1... | collective-permute-start | bytes 294920 | tf_op jit(solution)/shard_map/ppermute | solution.py:28
  15.4 4.9 %all-to-all-start = ((bf16[8,48,1024]{2,1,0:T(8,128)(2,1)}), bf16[8,48,1024]{2,1,0:T(8,128)(2,1)S(1)}, u32[]{:S(2)}, u32[]{:S(2)}) async-start(bf16[8,48,1024]{2,1,0:T(8,128)(2,1)} %bitcast.4), calls=%async_computation | async-start | bytes 1572864 | tf_op jit(solution)/shard_map/all_to_all | solution.py:131
  22.1 18.3 %all-reduce = s32[64]{0:T(128)S(1)} all-reduce(s32[64]{0:T(128)S(1)} %dynamic-update-slice), channel_id=2, replica_groups=mesh['dp'=4,'expert'=8] {'expert'}, use_global_device_ids=true, to_apply=%add | all-reduce | flops 64 | bytes 512
  43.8 4.6 %collective-permute-start.6 = (bf16[1,48,1024]{2,1,0:T(8,128)(2,1)S(1)}, bf16[1,48,1024]{2,1,0:T(8,128)(2,1)S(1)}, u32[]{:S(2)}, u32[]{:S(2)}) collective-permute-start(bf16[1,48,1024]{2,1,0:T(8,128)(2,1)S(1)} %get-tuple-element.155), channel_id=1, source_target_pairs={{0,7},{1,0},{2,1},{3,2},{4,3},{5,4},{6,5},{7,6},{8,15},{9,8},{10,9... | collective-permute-start | bytes 294920 | tf_op jit(solution)/shard_map/ppermute | solution.py:28
  48.5 3.6 %collective-permute-start.3 = (bf16[1,48,1024]{2,1,0:T(8,128)(2,1)S(1)}, bf16[1,48,1024]{2,1,0:T(8,128)(2,1)S(1)}, u32[]{:S(2)}, u32[]{:S(2)}) collective-permute-start(bf16[1,48,1024]{2,1,0:T(8,128)(2,1)S(1)} %get-tuple-element.158), channel_id=1, source_target_pairs={{0,4},{1,5},{2,6},{3,7},{4,0},{5,1},{6,2},{7,3},{8,12},{9,13},{10,... | collective-permute-start | bytes 294920 | tf_op jit(solution)/shard_map/ppermute | solution.py:28
  52.1 10.1 %collective-permute-done.2 = bf16[1,48,1024]{2,1,0:T(8,128)(2,1)S(1)} collective-permute-done((bf16[1,48,1024]{2,1,0:T(8,128)(2,1)S(1)}, bf16[1,48,1024]{2,1,0:T(8,128)(2,1)S(1)}, u32[]{:S(2)}, u32[]{:S(2)}) %collective-permute-start.2) | collective-permute-done | bytes 98336 | tf_op jit(solution)/shard_map/ppermute | solution.py:28
  62.6 2.9 %gather_fusion.1 = bf16[608,1024]{1,0:T(8,128)(2,1)S(1)} fusion(bf16[384,1024]{1,0:T(8,128)(2,1)S(1)} %bitcast.40, s32[1024]{0:T(1024)S(1)} %pad_clamp_fusion.1), kind=kCustom, calls=%fused_computation.2.clone | custom fusion | bytes 2492800 | tf_op jit(solution)/shard_map/jit(_take)/gather | solution.py:147
  65.5 3.5 %gather_fusion = bf16[608,1024]{1,0:T(8,128)(2,1)} fusion(bf16[384,1024]{1,0:T(8,128)(2,1)S(1)} %bitcast.42, s32[1024]{0:T(1024)S(1)} %pad_clamp_fusion.1), kind=kCustom, calls=%fused_computation.clone | custom fusion | bytes 2492800 | tf_op jit(solution)/shard_map/jit(_take)/gather | solution.py:144
  69.0 3.1 %select_select_fusion = (bf16[608,1024]{1,0:T(8,128)(2,1)}, bf16[608,1024]{1,0:T(8,128)(2,1)}) fusion(bf16[608,1024]{1,0:T(8,128)(2,1)S(1)} %gather_fusion.1, pred[608]{0:T(1024)(128)(4,1)S(1)} %get-tuple-element.151, pred[608]{0:T(1024)(128)(4,1)S(1)} %iota_compare_fusion.9, bf16[608,1024]{1,0:T(8,128)(2,1)} %gather_fusion), kind=kLoop, calls=%fused_computation.33 | loop fusion | flops 2490368 | bytes 4981952 | tf_op jit(solution)/shard_map/jit(_where)/select_n | solution.py:146
  75.6 5.8 %while.26 = (s32[]{:T(128)}, bf16[608,1024]{1,0:T(8,128)(2,1)}, bf16[608,1024]{1,0:T(8,128)(2,1)S(1)}, bf16[608,768]{1,0:T(8,128)(2,1)}, bf16[608,384]{1,0:T(8,1...) while((s32[]{:T(128)}, bf16[608,1024]{1,0:T(8,128)(2,1)}, ...), condition=%wide.region_11.13_spmd, body=%wide.region_10.12_spmd.sunk | while | flops 605962240 | bytes 11174119 | solution.py:108
  75.6 1.4 fusion.67
  81.4 2.7 %broadcast_in_dim.101 = f32[1024,1152]{0,1:T(8,128)} broadcast(f32[]{:T(128)} %constant.205.clone.1), dimensions={} | broadcast | bytes 4718596 | tf_op jit(solution)/shard_map/broadcast_in_dim | solution.py:189
  84.2 7.0 %while.27 = (s32[]{:T(128)}, f32[1024,1152]{0,1:T(8,128)}, s32[]{:T(128)}, bf16[608,1024]{1,0:T(8,128)(2,1)}, bf16[608,768]{1,0:T(8,128)(2,1)}, /*index=5*/bf16[...) while((s32[]{:T(128)}, f32[1024,1152]{0,1:T(8,128)}, ...), condition=%wide.region_15.18_spmd, body=%wide.region_14.17_spmd.sunk | while | flops 304349184 | bytes 57444560 | solution.py:188
  84.2 1.5 fusion.75
  85.7 1.6 fusion.76
  87.4 1.7 maximum_add_fusion.2
  89.1 2.1 %copy-done.2 = f32[1024,1152]{0,1:T(8,128)} copy-done((f32[1024,1152]{0,1:T(8,128)}, f32[1024,1152]{0,1:T(8,128)S(1)}, u32[]{:S(2)}) %copy-start.2) | copy-done | bytes 4718616 | tf_op jit(solution)/shard_map/while
  91.2 4.9 %copy.12 = bf16[1024,1152]{1,0:T(8,128)(2,1)} copy(f32[1024,1152]{0,1:T(8,128)} %get-tuple-element.105) | data formatting | bytes 7077888 | tf_op jit(solution)/shard_map/while | solution.py:188
  97.4 2.7 %gather_fusion.2 = bf16[384,1024]{1,0:T(8,128)(2,1)} fusion(bf16[608,1024]{1,0:T(8,128)(2,1)S(1)} %copy-done.4, s32[1024]{0:T(1024)S(1)} %pad_clamp_fusion), kind=kCustom, calls=%fused_computation.1.clone | custom fusion | bytes 1574400 | tf_op jit(solution)/shard_map/jit(_take)/gather | solution.py:164
  100.1 2.1 %gather_fusion.3 = bf16[384,1024]{1,0:T(8,128)(2,1)S(1)} fusion(bf16[608,1024]{1,0:T(8,128)(2,1)S(1)} %get-tuple-element.102, s32[1024]{0:T(1024)S(1)} %pad_clamp_fusion), kind=kCustom, calls=%fused_computation.3.clone | custom fusion | bytes 1574400 | tf_op jit(solution)/shard_map/jit(_take)/gather | solution.py:169
  103.3 48.2 %all_to_all.36 = bf16[8,48,1024]{2,1,0:T(8,128)(2,1)S(1)} all-to-all(bf16[8,48,1024]{2,1,0:T(8,128)(2,1)S(1)} %bitcast.46), channel_id=1, replica_groups=mesh['dp'=4,'expert'=8] {'expert'}, dimensions={0} | all-to-all | bytes 1572864 | tf_op jit(solution)/shard_map/all_to_all | solution.py:174
  151.6 3.8 %all-to-all-start.1 = ((bf16[8,48,1024]{2,1,0:T(8,128)(2,1)}), bf16[8,48,1024]{2,1,0:T(8,128)(2,1)S(1)}, u32[]{:S(2)}, u32[]{:S(2)}) async-start(bf16[8,48,1024]{2,1,0:T(8,128)(2,1)} %bitcast.10), calls=%async_computation.1 | async-start | bytes 1572864 | tf_op jit(solution)/shard_map/all_to_all | solution.py:173
  156.4 18.9 %all-to-all-done.1 = bf16[8,48,1024]{2,1,0:T(8,128)(2,1)S(1)} async-done(((bf16[8,48,1024]{2,1,0:T(8,128)(2,1)}), bf16[8,48,1024]{2,1,0:T(8,128)(2,1)S(1)}, u32[]{:S(2)}, u32[]{:S(2)}) %all-to-all-start.1) | async-done | bytes 786464 | tf_op jit(solution)/shard_map/all_to_all | solution.py:173
  175.3 1.7 fusion.19
  (80 shorter events, 23.2 us)
Async XLA Ops:
  7.2 7.0 %copy-start = (bf16[128,1024]{1,0:T(8,128)(2,1)S(1)}, bf16[128,1024]{1,0:T(8,128)(2,1)}, u32[]{:S(2)}) copy-start(bf16[128,1024]{1,0:T(8,128)(2,1)} %param.14) | copy-start | bytes 786436
  11.1 9.5 %copy-start.9 = (u32[32]{0:T(128)S(1)}, u32[32]{0:T(128)}, u32[]{:S(2)}) copy-start(u32[32]{0:T(128)} %constant.210) | copy-start | bytes 388
  11.1 32.0 %collective-permute-start = (bf16[1,48,1024]{2,1,0:T(8,128)(2,1)S(1)}, bf16[1,48,1024]{2,1,0:T(8,128)(2,1)S(1)}, u32[]{:S(2)}, u32[]{:S(2)}) collective-permute-start(bf16[1,48,1024]{2,1,0:T(8,128)(2,1)S(1)} %constant_dynamic-slice_fusion.6), channel_id=1, source_target_pairs={{0,1},{1,2},{2,3},{3,4},{4,5},{5,6},{6,7},{7,0},{8,9},{9,10},{10,1... | collective-permute-start | bytes 294920 | tf_op jit(solution)/shard_map/ppermute | solution.py:28
  15.4 50.1 %all-to-all-start = ((bf16[8,48,1024]{2,1,0:T(8,128)(2,1)}), bf16[8,48,1024]{2,1,0:T(8,128)(2,1)S(1)}, u32[]{:S(2)}, u32[]{:S(2)}) async-start(bf16[8,48,1024]{2,1,0:T(8,128)(2,1)} %bitcast.4), calls=%async_computation | async-start | bytes 1572864 | tf_op jit(solution)/shard_map/all_to_all | solution.py:131
  20.3 156.7 %reduce-scatter.2.cloned.1.call-start = ((), (), s32[]{:S(2)}) async-start(), calls=%async_computation.4 | async-start | bytes 2949120 | tf_op jit(solution)/shard_map/reduce_scatter | solution.py:187
  43.1 9.0 %collective-permute-start.1 = (bf16[1,48,1024]{2,1,0:T(8,128)(2,1)S(1)}, bf16[1,48,1024]{2,1,0:T(8,128)(2,1)S(1)}, u32[]{:S(2)}, u32[]{:S(2)}) collective-permute-start(bf16[1,48,1024]{2,1,0:T(8,128)(2,1)S(1)} %get-tuple-element.160), channel_id=1, source_target_pairs={{0,2},{1,3},{2,4},{3,5},{4,6},{5,7},{6,0},{7,1},{8,10},{9,11},{10,... | collective-permute-start | bytes 294920 | tf_op jit(solution)/shard_map/ppermute | solution.py:28
  43.8 18.7 %collective-permute-start.6 = (bf16[1,48,1024]{2,1,0:T(8,128)(2,1)S(1)}, bf16[1,48,1024]{2,1,0:T(8,128)(2,1)S(1)}, u32[]{:S(2)}, u32[]{:S(2)}) collective-permute-start(bf16[1,48,1024]{2,1,0:T(8,128)(2,1)S(1)} %get-tuple-element.155), channel_id=1, source_target_pairs={{0,7},{1,0},{2,1},{3,2},{4,3},{5,4},{6,5},{7,6},{8,15},{9,8},{10,9... | collective-permute-start | bytes 294920 | tf_op jit(solution)/shard_map/ppermute | solution.py:28
  48.5 14.1 %collective-permute-start.5 = (bf16[1,48,1024]{2,1,0:T(8,128)(2,1)S(1)}, bf16[1,48,1024]{2,1,0:T(8,128)(2,1)S(1)}, u32[]{:S(2)}, u32[]{:S(2)}) collective-permute-start(bf16[1,48,1024]{2,1,0:T(8,128)(2,1)S(1)} %get-tuple-element.156), channel_id=1, source_target_pairs={{0,6},{1,7},{2,0},{3,1},{4,2},{5,3},{6,4},{7,5},{8,14},{9,15},{10,... | collective-permute-start | bytes 294920 | tf_op jit(solution)/shard_map/ppermute | solution.py:28
  48.5 14.0 %collective-permute-start.4 = (bf16[1,48,1024]{2,1,0:T(8,128)(2,1)S(1)}, bf16[1,48,1024]{2,1,0:T(8,128)(2,1)S(1)}, u32[]{:S(2)}, u32[]{:S(2)}) collective-permute-start(bf16[1,48,1024]{2,1,0:T(8,128)(2,1)S(1)} %get-tuple-element.157), channel_id=1, source_target_pairs={{0,5},{1,6},{2,7},{3,0},{4,1},{5,2},{6,3},{7,4},{8,13},{9,14},{10,... | collective-permute-start | bytes 294920 | tf_op jit(solution)/shard_map/ppermute | solution.py:28
  48.5 14.0 %collective-permute-start.3 = (bf16[1,48,1024]{2,1,0:T(8,128)(2,1)S(1)}, bf16[1,48,1024]{2,1,0:T(8,128)(2,1)S(1)}, u32[]{:S(2)}, u32[]{:S(2)}) collective-permute-start(bf16[1,48,1024]{2,1,0:T(8,128)(2,1)S(1)} %get-tuple-element.158), channel_id=1, source_target_pairs={{0,4},{1,5},{2,6},{3,7},{4,0},{5,1},{6,2},{7,3},{8,12},{9,13},{10,... | collective-permute-start | bytes 294920 | tf_op jit(solution)/shard_map/ppermute | solution.py:28
  52.1 10.1 %collective-permute-start.2 = (bf16[1,48,1024]{2,1,0:T(8,128)(2,1)S(1)}, bf16[1,48,1024]{2,1,0:T(8,128)(2,1)S(1)}, u32[]{:S(2)}, u32[]{:S(2)}) collective-permute-start(bf16[1,48,1024]{2,1,0:T(8,128)(2,1)S(1)} %get-tuple-element.159), channel_id=1, source_target_pairs={{0,3},{1,4},{2,5},{3,6},{4,7},{5,0},{6,1},{7,2},{8,11},{9,12},{10,... | collective-permute-start | bytes 294920 | tf_op jit(solution)/shard_map/ppermute | solution.py:28
  73.8 1.8 copy-start.3
  75.6 1.4 copy-start.5
  84.2 3.2 %copy-start.1 = (f32[1024,1152]{0,1:T(8,128)S(1)}, f32[1024,1152]{0,1:T(8,128)}, u32[]{:S(2)}) copy-start(f32[1024,1152]{0,1:T(8,128)} %get-tuple-element.336) | copy-start | bytes 14155780 | tf_op jit(solution)/shard_map/while
  89.0 2.1 %copy-start.2 = (f32[1024,1152]{0,1:T(8,128)}, f32[1024,1152]{0,1:T(8,128)S(1)}, u32[]{:S(2)}) copy-start(f32[1024,1152]{0,1:T(8,128)S(1)} %maximum_add_fusion.2) | copy-start | bytes 14155780 | tf_op jit(solution)/shard_map/while
  96.1 1.3 copy-start.4
  100.1 2.1 %copy-start.6 = (bf16[384,1024]{1,0:T(8,128)(2,1)S(1)}, bf16[384,1024]{1,0:T(8,128)(2,1)}, u32[]{:S(2)}) copy-start(bf16[384,1024]{1,0:T(8,128)(2,1)} %gather_fusion.2) | copy-start | bytes 2359300
  151.6 23.7 %copy-start.7 = (bf16[128,1024]{1,0:T(8,128)(2,1)S(1)}, bf16[128,1024]{1,0:T(8,128)(2,1)}, u32[]{:S(2)}) copy-start(bf16[128,1024]{1,0:T(8,128)(2,1)} %param.19) | copy-start | bytes 786436
  151.6 23.7 %copy-start.8 = (f32[128]{0:T(128)S(1)}, f32[128]{0:T(128)}, u32[]{:S(2)}) copy-start(f32[128]{0:T(128)} %param.16) | copy-start | bytes 1540
  151.6 23.7 %all-to-all-start.1 = ((bf16[8,48,1024]{2,1,0:T(8,128)(2,1)}), bf16[8,48,1024]{2,1,0:T(8,128)(2,1)S(1)}, u32[]{:S(2)}, u32[]{:S(2)}) async-start(bf16[8,48,1024]{2,1,0:T(8,128)(2,1)} %bitcast.10), calls=%async_computation.1 | async-start | bytes 1572864 | tf_op jit(solution)/shard_map/all_to_all | solution.py:173
Sparse Core Ops, SparseCore 0:
  96.3 56.3 reduce-scatter.1
